TPU v7x, 32 devices: a whole 2x2x4 slice. The times are simulated.
32 devices in a mesh: fsdp: 8 (over z, x), rep: 4 (over y, core).
Axes of the slice: x: 2, y: 2, z: 4, core: 2. Of those that a mesh axis runs over, the one named last changes fastest.
Arguments:
- samples: bfloat16 [768, 4096], P(('fsdp', 'rep')), may hold values from -10 to 10
- dual_weight: bfloat16 [8192, 4096], P('fsdp'), may hold values from -0.09375 to 0.09375
- dual_vector: float32 [2, 8192], P(None, 'fsdp'), may hold values from 0 to 2
- map_weight: float32 [8192, 4096], P(('fsdp', 'rep')), may hold values from -0.09375 to 0.09375
- map_vector: float32 [2, 8192], P(None, ('fsdp', 'rep')), may hold values from 0.001 to 2
- moment_weight: float32 [8192, 4096], P(('fsdp', 'rep')), may hold values from -0.006 to 0.006
- square_weight: float32 [8192, 4096], P(('fsdp', 'rep')), may hold values from 0.0001 to 0.01
- moment_vector: float32 [2, 8192], P(None, ('fsdp', 'rep')), may hold values from -0.03 to 0.03
- square_vector: float32 [2, 8192], P(None, ('fsdp', 'rep')), may hold values from 0.0001 to 0.01
Outputs:
- next_weight: float32 [8192, 4096], P(('fsdp', 'rep'))
- next_vector: float32 [2, 8192], P(None, ('fsdp', 'rep'))
- next_moment_weight: float32 [8192, 4096], P(('fsdp', 'rep'))
- next_square_weight: float32 [8192, 4096], P(('fsdp', 'rep'))
- next_moment_vector: float32 [2, 8192], P(None, ('fsdp', 'rep'))
- next_square_vector: float32 [2, 8192], P(None, ('fsdp', 'rep'))
All inputs are finite; a program needn't handle non-finite values.
Results may differ from a plain program's by a relative error of at most 0.004.
Values may be sent and summed in bfloat16 or wider, within the bound.
A program may use at most 128 MiB of HBM per device.

v0:
```python
import jax
import jax.numpy as jnp
from jax import lax
from jax.sharding import PartitionSpec as P

beta_one = 0.9
beta_two = 0.999
learn_rate = 0.001
epsilon = 1e-08
adam_step = 10


def contract_last(left, right):
    return lax.dot_general(
        left, right, (((1,), (1,)), ((), ())), preferred_element_type=jnp.float32
    )


def contract_first(left, right):
    return lax.dot_general(
        left, right, (((0,), (0,)), ((), ())), preferred_element_type=jnp.float32
    )


def adam_update(param, grad, moment, square):
    moment_new = beta_one * moment + (1.0 - beta_one) * grad
    square_new = beta_two * square + (1.0 - beta_two) * grad * grad
    fix_one = 1.0 - beta_one**adam_step
    fix_two = 1.0 - beta_two**adam_step
    update = learn_rate * (moment_new / fix_one) / (jnp.sqrt(square_new / fix_two) + epsilon)
    return (param - update, moment_new, square_new)


def body(
    samples,
    dual_weight,
    dual_vector,
    map_weight,
    map_vector,
    moment_weight,
    square_weight,
    moment_vector,
    square_vector,
):
    group_rows = lax.all_gather(samples, "fsdp", axis=0, tiled=True)
    weight_slab, vector_slab = (
        lax.all_gather(map_weight.astype(jnp.bfloat16), "rep", axis=0, tiled=True),
        lax.all_gather(map_vector.astype(jnp.bfloat16), "rep", axis=1, tiled=True),
    )
    readout = vector_slab[0].astype(jnp.float32)
    offset = vector_slab[1].astype(jnp.float32)
    inverse_rows = 1.0 / (group_rows.shape[0] * lax.axis_size("rep"))
    hidden = contract_last(group_rows, weight_slab) + offset
    sigma = jax.nn.sigmoid(hidden)
    scaled = (readout * sigma).astype(jnp.bfloat16)
    group_float = group_rows.astype(jnp.float32)
    mapped = group_float + lax.psum(
        jnp.dot(scaled, weight_slab, preferred_element_type=jnp.float32).astype(jnp.bfloat16),
        "fsdp",
    ).astype(jnp.float32)
    mapped_low = mapped.astype(jnp.bfloat16)
    dual_hidden = contract_last(mapped_low, dual_weight) + dual_vector[1]
    dual_scaled = (dual_vector[0] * jax.nn.sigmoid(dual_hidden)).astype(jnp.bfloat16)
    dual_grad = mapped + lax.psum(
        jnp.dot(dual_scaled, dual_weight, preferred_element_type=jnp.float32).astype(jnp.bfloat16),
        "fsdp",
    ).astype(jnp.float32)
    residual = (group_float - dual_grad).astype(jnp.bfloat16)
    pulled = contract_last(residual, weight_slab)
    slope = sigma * (1.0 - sigma)
    curve_float = readout * slope * pulled
    curve_term = curve_float.astype(jnp.bfloat16)
    left_stack = jnp.concatenate([scaled, curve_term], axis=0)
    right_stack = jnp.concatenate([residual, group_rows], axis=0)
    grad_slab = contract_first(left_stack, right_stack) * inverse_rows
    grad_small = (
        jnp.stack([jnp.sum(sigma * pulled, axis=0), jnp.sum(curve_float, axis=0)]) * inverse_rows
    )
    owner_weight, owner_vector = (
        lax.psum_scatter(grad_slab, "rep", scatter_dimension=0, tiled=True),
        lax.psum_scatter(grad_small, "rep", scatter_dimension=1, tiled=True),
    )
    next_weight, next_moment_weight, next_square_weight = adam_update(
        map_weight, owner_weight, moment_weight, square_weight
    )
    raw_vector, next_moment_vector, next_square_vector = adam_update(
        map_vector, owner_vector, moment_vector, square_vector
    )
    next_vector = jnp.concatenate([jnp.maximum(raw_vector[0:1], 0.0), raw_vector[1:2]], axis=0)
    return (
        next_weight,
        next_vector,
        next_moment_weight,
        next_square_weight,
        next_moment_vector,
        next_square_vector,
    )


def solution(mesh):
    return jax.shard_map(
        body,
        mesh=mesh,
        in_specs=(
            P(("fsdp", "rep"), None),
            P("fsdp", None),
            P(None, "fsdp"),
            P(("fsdp", "rep"), None),
            P(None, ("fsdp", "rep")),
            P(("fsdp", "rep"), None),
            P(("fsdp", "rep"), None),
            P(None, ("fsdp", "rep")),
            P(None, ("fsdp", "rep")),
        ),
        out_specs=(
            P(("fsdp", "rep"), None),
            P(None, ("fsdp", "rep")),
            P(("fsdp", "rep"), None),
            P(("fsdp", "rep"), None),
            P(None, ("fsdp", "rep")),
            P(None, ("fsdp", "rep")),
        ),
        check_vma=False,
    )
```

profile of v0, /device:TPU:0, one launch (start us, length us, event | category | flops | bytes accessed | tf_op | source)
XLA Modules:
  0.0 494.8 jit_solution(3073785880574631769)
XLA Ops:
  7.2 0.0 all-gather.3.cloned.1.call-start
  7.2 0.7 all-gather.3.cloned.1.call-update
  7.9 0.0 copy-start.1
  7.9 0.0 all-gather.5.cloned.1.call-start
  8.0 3.8 convert_element_type.41
  11.8 0.0 all-gather.5.cloned.1.call-update
  11.8 0.0 all-reduce.3.cloned.1.call-start
  11.8 0.0 copy-done.1
  11.8 6.0 %all_gather.9 = bf16[2,1024]{1,0:T(2,128)(2,1)S(1)} all-gather(bf16[2,256]{1,0:T(2,128)(2,1)S(1)} %convert_element_type.40), channel_id=1, replica_groups=mesh['fsdp'=8,'rep'=4] {'rep'}, dimensions={1}, use_global_device_ids=true | all-gather | bytes 5120 | tf_op jit(solution)/shard_map/all_gather | solution.py:48
  17.9 39.2 %all-gather.3.cloned.1.call-done = bf16[192,4096]{1,0:T(8,128)(2,1)} async-done(((bf16[24,4096]{1,0:T(8,128)(2,1)}), bf16[192,4096]{1,0:T(8,128)(2,1)}) %all-gather.3.cloned.1.call-update) | async-done | bytes 1572880 | tf_op jit(solution)/shard_map/all_gather | solution.py:45
  57.1 58.8 %all-gather.5.cloned.1.call-done = bf16[1024,4096]{1,0:T(8,128)(2,1)} async-done(((bf16[256,4096]{1,0:T(8,128)(2,1)}), bf16[1024,4096]{1,0:T(8,128)(2,1)}) %all-gather.5.cloned.1.call-update) | async-done | bytes 8388624 | tf_op jit(solution)/shard_map/all_gather | solution.py:47
  115.9 0.0 copy-start.5
  115.9 7.9 %multiply_convert_fusion = (bf16[192,1024]{1,0:T(8,128)(2,1)S(1)}, f32[192,1024]{1,0:T(8,128)}) fusion(f32[1024]{0:T(1024)S(1)} %bitcast.18, f32[1024]{0:T(1024)S(1)} %bitcast.20, bf16[192,4096]{1,0:T(8,128)(2,1)} %all-gather.3.cloned.1.call-done, bf16[1024,4096]{1,0:T(8,128)(2,1)} %all-gather.5.cloned.1.call-done), kind=kOutput, calls=%fused_computation.34 | convolution fusion | flops 1611792384 | bytes 11149312 | tf_op jit(solution)/shard_map/dot_general | solution.py:14
  123.8 0.0 copy-done.5
  123.8 0.0 copy-start.2
  123.8 0.0 copy-start
  123.8 3.0 convolution_convert_fusion.1
  126.8 0.0 all-reduce.3.cloned.1.call-update
  126.8 0.0 all-reduce.5.cloned.1.call-start
  126.9 0.0 copy-done.2
  126.9 89.3 %all-reduce.3.cloned.1.call-done = bf16[192,4096]{1,0:T(8,128)(2,1)} async-done(((bf16[192,4096]{1,0:T(8,128)(2,1)}), bf16[192,4096]{1,0:T(8,128)(2,1)}) %all-reduce.3.cloned.1.call-update) | async-done | bytes 1572880 | tf_op jit(solution)/shard_map/psum | solution.py:57
  216.2 0.0 copy-done
  216.2 12.0 %convolution_convert_fusion = bf16[192,4096]{1,0:T(8,128)(2,1)} fusion(bf16[1024,4096]{1,0:T(8,128)(2,1)} %param.10, bf16[192,4096]{1,0:T(8,128)(2,1)} %all-reduce.3.cloned.1.call-done, bf16[192,4096]{1,0:T(8,128)(2,1)S(1)} %copy-done, f32[1024]{0:T(1024)S(1)} %bitcast.22, f32[1024]{0:T(1024)S(1)} %bitcast.21), kind=kOutput, calls=%fused_computation.2 | convolution fusion | flops 3226337280 | bytes 13115392 | tf_op jit(solution)/shard_map/dot_general | solution.py:65
  228.2 0.0 all-reduce.5.cloned.1.call-update
  228.2 0.0 reduce-scatter.7.cloned.1.call-start
  228.3 88.6 %all-reduce.5.cloned.1.call-done = bf16[192,4096]{1,0:T(8,128)(2,1)} async-done(((bf16[192,4096]{1,0:T(8,128)(2,1)}), bf16[192,4096]{1,0:T(8,128)(2,1)}) %all-reduce.5.cloned.1.call-update) | async-done | bytes 1572880 | tf_op jit(solution)/shard_map/psum | solution.py:64
  316.9 2.7 fusion.1
  319.6 7.2 %multiply_reduce_fusion = (f32[1024]{0:T(1024)S(1)}, f32[1024]{0:T(1024)S(1)}, bf16[192,1024]{1,0:T(8,128)(2,1)}) fusion(f32[192,1024]{1,0:T(8,128)} %get-tuple-element.22, f32[1024]{0:T(1024)S(1)} %bitcast.19, bf16[192,4096]{1,0:T(8,128)(2,1)S(1)} %fusion.1, bf16[1024,4096]{1,0:T(8,128)(2,1)} %all-gather.5.cloned.1.call-done), kind=kOutput, calls=%fused_computation.33 | convolution fusion | flops 1612183552 | bytes 11153408 | tf_op jit(solution)/shard_map/dot_general | solution.py:14
  326.9 1.0 copy.15
  327.9 0.0 reduce-scatter.7.cloned.1.call-update
  327.9 0.2 reduce-scatter.5.cloned.1.call-start
  328.1 9.2 %convolution_multiply_fusion = f32[1024,4096]{1,0:T(8,128)} fusion(bf16[192,4096]{1,0:T(8,128)(2,1)S(1)} %copy-done, bf16[192,4096]{1,0:T(8,128)(2,1)S(1)} %fusion.1, bf16[192,1024]{1,0:T(8,128)(2,1)} %get-tuple-element.14, bf16[192,1024]{1,0:T(8,128)(2,1)S(1)} %get-tuple-element.21), kind=kOutput, calls=%fused_computation | convolution fusion | flops 3233284096 | bytes 20709376 | tf_op jit(solution)/shard_map/dot_general | solution.py:20
  337.4 0.0 copy-start.3
  337.4 0.0 copy-start.4
  337.4 0.0 reduce-scatter.5.cloned.1.call-update
  337.4 11.6 %reduce-scatter.7.cloned.1.call-done = f32[256,2]{1,0:T(8,128)} async-done(((f32[1024,2]{1,0:T(8,128)}), f32[256,2]{1,0:T(8,128)}) %reduce-scatter.7.cloned.1.call-update) | async-done | bytes 2064
  349.0 1.0 copy.16
  350.0 0.0 copy-done.3
  350.0 0.0 copy-done.4
  350.0 0.6 divide_subtract_fusion.1
  350.6 0.6 pad_maximum_fusion
  351.2 125.3 %reduce-scatter.5.cloned.1.call-done = f32[256,4096]{1,0:T(8,128)} async-done(((f32[1024,4096]{1,0:T(8,128)}), f32[256,4096]{1,0:T(8,128)}) %reduce-scatter.5.cloned.1.call-update) | async-done | bytes 4194320 | tf_op jit(solution)/shard_map/reduce_scatter | solution.py:80
  476.5 11.4 %divide_subtract_fusion = (f32[256,4096]{1,0:T(8,128)}, f32[256,4096]{1,0:T(8,128)}, f32[256,4096]{1,0:T(8,128)}) fusion(f32[256,4096]{1,0:T(8,128)} %param.12, f32[256,4096]{1,0:T(8,128)} %reduce-scatter.5.cloned.1.call-done, f32[256,4096]{1,0:T(8,128)} %param.14, f32[256,4096]{1,0:T(8,128)} %param.15), kind=kLoop, calls=%fused_computation.5 | loop fusion | flops 12582912 | bytes 29360128 | tf_op jit(solution)/shard_map/sub | solution.py:31
  (5 shorter events, 0.0 us)
Async XLA Ops:
  7.2 49.9 %all-gather.3.cloned.1.call-start = ((), (), s32[]{:S(2)}) async-start(), calls=%async_computation.2 | async-start | bytes 1769472 | tf_op jit(solution)/shard_map/all_gather | solution.py:45
  7.9 3.9 copy-start.1
  7.9 108.0 %all-gather.5.cloned.1.call-start = ((), (), s32[]{:S(2)}) async-start(), calls=%async_computation.3 | async-start | bytes 10485760 | tf_op jit(solution)/shard_map/all_gather | solution.py:47
  11.8 204.5 %all-reduce.3.cloned.1.call-start = ((), (), s32[]{:S(2)}) async-start(), calls=%async_computation.4 | async-start | bytes 3145728 | tf_op jit(solution)/shard_map/psum | solution.py:57
  115.9 7.9 %copy-start.5 = (bf16[1024,4096]{1,0:T(8,128)(2,1)S(1)}, bf16[1024,4096]{1,0:T(8,128)(2,1)}, u32[]{:S(2)}) copy-start(bf16[1024,4096]{1,0:T(8,128)(2,1)} %all-gather.5.cloned.1.call-done) | copy-start | bytes 25165828
  123.8 3.1 copy-start.2
  123.8 92.5 %copy-start = (bf16[192,4096]{1,0:T(8,128)(2,1)S(1)}, bf16[192,4096]{1,0:T(8,128)(2,1)}, u32[]{:S(2)}) copy-start(bf16[192,4096]{1,0:T(8,128)(2,1)} %all-gather.3.cloned.1.call-done) | copy-start | bytes 4718596
  126.8 190.1 %all-reduce.5.cloned.1.call-start = ((), (), s32[]{:S(2)}) async-start(), calls=%async_computation.5 | async-start | bytes 3145728 | tf_op jit(solution)/shard_map/psum | solution.py:64
  228.2 120.8 %reduce-scatter.7.cloned.1.call-start = ((), (), s32[]{:S(2)}) async-start(), calls=%async_computation.7 | async-start | bytes 655360
  327.9 148.6 %reduce-scatter.5.cloned.1.call-start = ((), (), s32[]{:S(2)}) async-start(), calls=%async_computation.6 | async-start | bytes 20971520 | tf_op jit(solution)/shard_map/reduce_scatter | solution.py:80
  337.4 12.6 %copy-start.3 = (f32[2,256]{1,0:T(2,128)S(1)}, f32[2,256]{1,0:T(2,128)}, u32[]{:S(2)}) copy-start(f32[2,256]{1,0:T(2,128)} %param.16) | copy-start | bytes 6148
  337.4 12.6 %copy-start.4 = (f32[2,256]{1,0:T(2,128)S(1)}, f32[2,256]{1,0:T(2,128)}, u32[]{:S(2)}) copy-start(f32[2,256]{1,0:T(2,128)} %param.17) | copy-start | bytes 6148
Sparse Core Ops, SparseCore 0:
  10.2 46.8 all-gather.2
  59.2 56.6 all-gather.4
  126.9 89.2 all-reduce.2
  228.4 88.5 all-reduce.4
  328.0 20.9 reduce-scatter.6
  351.4 125.0 reduce-scatter.4
where the time goes:
time: 495 us
  waiting for transfers between devices  414 us (84%)
  matrix products  39.3 us (8%)
  other arithmetic  19.1 us (4%)
  between operations  14.2 us (3%)
  blocking collectives  6.04 us (1%)
    reduce_scatter x1, waiting for transfers between devices, body(): lax.psum_scatter(grad_slab, 'rep', scatter_dimension=0, tiled=True)  125 us
    psum x1, waiting for transfers between devices, body(): lax.psum(jnp.dot(scaled, weight_slab, preferred_element_type=jnp.float32)...  89.3 us
    psum x1, waiting for transfers between devices, body(): lax.psum(jnp.dot(dual_scaled, dual_weight, preferred_element_type=jnp.flo...  88.6 us
    all_gather x1, waiting for transfers between devices, body(): lax.all_gather(map_weight.astype(jnp.bfloat16), 'rep', axis=0, tiled=True)  58.8 us
    all_gather x1, waiting for transfers between devices, body(): group_rows = lax.all_gather(samples, 'fsdp', axis=0, tiled=True)  39.2 us
    dot_general x2, matrix products, contract_last(): lax.dot_general(left, right, (((1,), (1,)), ((), ())), preferred_element_...  15.1 us
    unnamed x7, waiting for transfers between devices  12.4 us
    sub x2, other arithmetic, adam_update(): return (param - update, moment_new, square_new)  12 us
  transfers between devices with their start and end apart: 6, of which 6 were waited for; matrix products, arithmetic and copies ran while one was open for 3% of the time, Pallas kernels for 0%

commit v1 on v0

--- a/solution.py
+++ b/solution.py
@@ -54,9 +54,12 @@
     sigma = jax.nn.sigmoid(hidden)
     scaled = (readout * sigma).astype(jnp.bfloat16)
     group_float = group_rows.astype(jnp.float32)
-    mapped = group_float + lax.psum(
-        jnp.dot(scaled, weight_slab, preferred_element_type=jnp.float32).astype(jnp.bfloat16),
-        "fsdp",
+    mapped = group_float + jnp.sum(
+        lax.all_gather(
+            jnp.dot(scaled, weight_slab, preferred_element_type=jnp.float32).astype(jnp.bfloat16),
+            axis_name="fsdp",
+        ),
+        axis=0,
     ).astype(jnp.float32)
     mapped_low = mapped.astype(jnp.bfloat16)
     dual_hidden = contract_last(mapped_low, dual_weight) + dual_vector[1]

time: 495 us -> 588 us (1.19)
  waiting for transfers between devices: 414 us -> 499 us
  other arithmetic: 19.1 us -> 26.4 us
    all_gather x0 -> x1, waiting for transfers between devices: none -> 176 us  [body(): lax.all_gather(jnp.dot(scaled, weight_slab, preferred_element_type=jnp.fl...]
    psum x1 -> x0, waiting for transfers between devices: 89.3 us -> none  [body(): lax.psum(jnp.dot(scaled, weight_slab, preferred_element_type=jnp.float32)...]
    reduce_sum x0 -> x1, other arithmetic: none -> 7.15 us  [body(): jnp.sum(lax.all_gather(jnp.dot(scaled, weight_slab, preferred_element_typ...]
where the time goes in v1:
time: 588 us
  waiting for transfers between devices  499 us (85%)
  matrix products  39.4 us (7%)
  other arithmetic  26.4 us (4%)
  between operations  14.2 us (2%)
  blocking collectives  6.04 us (1%)
    all_gather x1, waiting for transfers between devices, body(): lax.all_gather(jnp.dot(scaled, weight_slab, preferred_element_type=jnp.fl...  176 us
    reduce_scatter x1, waiting for transfers between devices, body(): lax.psum_scatter(grad_slab, 'rep', scatter_dimension=0, tiled=True)  125 us
    psum x1, waiting for transfers between devices, body(): lax.psum(jnp.dot(dual_scaled, dual_weight, preferred_element_type=jnp.flo...  87.4 us
    all_gather x1, waiting for transfers between devices, body(): lax.all_gather(map_weight.astype(jnp.bfloat16), 'rep', axis=0, tiled=True)  58.8 us
    all_gather x1, waiting for transfers between devices, body(): group_rows = lax.all_gather(samples, 'fsdp', axis=0, tiled=True)  39.2 us
    dot_general x2, matrix products, contract_last(): lax.dot_general(left, right, (((1,), (1,)), ((), ())), preferred_element_...  15 us
    unnamed x7, waiting for transfers between devices  12.5 us
    dot_general x1, matrix products, body(): jnp.dot(dual_scaled, dual_weight, preferred_element_type=jnp.float32)  12.1 us
  transfers between devices with their start and end apart: 6, of which 6 were waited for; matrix products, arithmetic and copies ran while one was open for 3% of the time, Pallas kernels for 0%

profile of v1, /device:TPU:0, one launch (start us, length us, event | category | flops | bytes accessed | tf_op | source)
XLA Modules:
  0.0 587.8 jit_solution(11808772259298278218)
XLA Ops:
  7.2 0.0 all-gather.5.cloned.1.call-start
  7.2 0.7 all-gather.5.cloned.1.call-update
  7.9 0.0 copy-start.2
  7.9 0.0 all-gather.7.cloned.1.call-start
  8.0 3.8 convert_element_type.43
  11.8 0.0 all-gather.7.cloned.1.call-update
  11.8 0.0 all-gather.9.cloned.1.call-start
  11.8 0.0 copy-done.2
  11.8 6.0 %all_gather.15 = bf16[2,1024]{1,0:T(2,128)(2,1)S(1)} all-gather(bf16[2,256]{1,0:T(2,128)(2,1)S(1)} %convert_element_type.42), channel_id=1, replica_groups=mesh['fsdp'=8,'rep'=4] {'rep'}, dimensions={1}, use_global_device_ids=true | all-gather | bytes 5120 | tf_op jit(solution)/shard_map/all_gather | solution.py:48
  17.9 39.2 %all-gather.5.cloned.1.call-done = bf16[192,4096]{1,0:T(8,128)(2,1)} async-done(((bf16[24,4096]{1,0:T(8,128)(2,1)}), bf16[192,4096]{1,0:T(8,128)(2,1)}) %all-gather.5.cloned.1.call-update) | async-done | bytes 1572880 | tf_op jit(solution)/shard_map/all_gather | solution.py:45
  57.1 58.8 %all-gather.7.cloned.1.call-done = bf16[1024,4096]{1,0:T(8,128)(2,1)} async-done(((bf16[256,4096]{1,0:T(8,128)(2,1)}), bf16[1024,4096]{1,0:T(8,128)(2,1)}) %all-gather.7.cloned.1.call-update) | async-done | bytes 8388624 | tf_op jit(solution)/shard_map/all_gather | solution.py:47
  115.9 0.0 copy-start.8
  115.9 7.9 %multiply_convert_fusion = (bf16[192,1024]{1,0:T(8,128)(2,1)S(1)}, f32[192,1024]{1,0:T(8,128)}) fusion(f32[1024]{0:T(1024)S(1)} %bitcast.20, f32[1024]{0:T(1024)S(1)} %bitcast.22, bf16[192,4096]{1,0:T(8,128)(2,1)} %all-gather.5.cloned.1.call-done, bf16[1024,4096]{1,0:T(8,128)(2,1)} %all-gather.7.cloned.1.call-done), kind=kOutput, calls=%fused_computation.34 | convolution fusion | flops 1611792384 | bytes 11149312 | tf_op jit(solution)/shard_map/dot_general | solution.py:14
  123.8 0.0 copy-done.8
  123.8 0.0 copy-start.3
  123.8 3.0 convolution_convert_fusion.1
  126.8 0.0 all-gather.9.cloned.1.call-update
  126.8 0.0 all-reduce.2.cloned.1.call-start
  126.9 0.0 copy-done.3
  126.9 0.6 fusion.50
  127.5 175.6 %all-gather.9.cloned.1.call-done = bf16[1536,4096]{1,0:T(8,128)(2,1)} async-done(((bf16[192,4096]{1,0:T(8,128)(2,1)}), bf16[1536,4096]{1,0:T(8,128)(2,1)}) %all-gather.9.cloned.1.call-update) | async-done | bytes 12582928 | tf_op jit(solution)/shard_map/all_gather | solution.py:58
  303.1 0.0 copy-start
  303.1 7.2 %reduce_sum.30 = bf16[192,4096]{1,0:T(8,128)(2,1)S(1)} reduce(bf16[8,192,4096]{2,1,0:T(8,128)(2,1)} %bitcast.17, bf16[]{:T(256)} %constant.13.clone.1), dimensions={0}, to_apply=%region_0.0 | reduce | flops 5505024 | bytes 14155778 | tf_op jit(solution)/shard_map/reduce_sum | solution.py:57
  310.2 0.0 copy-start.1
  310.2 0.0 copy-done
  310.2 0.0 copy-done.4
  310.3 0.0 copy-done.5
  310.3 12.1 %convolution_convert_fusion = bf16[192,4096]{1,0:T(8,128)(2,1)} fusion(bf16[1024,4096]{1,0:T(8,128)(2,1)} %param.10, bf16[192,4096]{1,0:T(8,128)(2,1)S(1)} %reduce_sum.30, bf16[192,4096]{1,0:T(8,128)(2,1)S(1)} %copy-done, f32[1024]{0:T(1024)S(1)} %bitcast.24, f32[1024]{0:T(1024)S(1)} %bitcast.23), kind=kOutput, calls=%fused_computation.2 | convolution fusion | flops 3226337280 | bytes 13115392 | tf_op jit(solution)/shard_map/dot_general | solution.py:68
  322.3 0.0 copy-done.1
  322.3 0.0 all-reduce.2.cloned.1.call-update
  322.4 0.2 reduce-scatter.7.cloned.1.call-start
  322.6 87.4 %all-reduce.2.cloned.1.call-done = bf16[192,4096]{1,0:T(8,128)(2,1)} async-done(((bf16[192,4096]{1,0:T(8,128)(2,1)}), bf16[192,4096]{1,0:T(8,128)(2,1)}) %all-reduce.2.cloned.1.call-update) | async-done | bytes 1572880 | tf_op jit(solution)/shard_map/psum | solution.py:67
  410.0 2.8 fusion.1
  412.8 0.0 copy-done.9
  412.8 7.1 %multiply_reduce_fusion = (f32[1024]{0:T(1024)S(1)}, f32[1024]{0:T(1024)S(1)}, bf16[192,1024]{1,0:T(8,128)(2,1)}) fusion(f32[192,1024]{1,0:T(8,128)S(1)} %copy-done.9, f32[1024]{0:T(1024)S(1)} %bitcast.21, bf16[192,4096]{1,0:T(8,128)(2,1)S(1)} %fusion.1, bf16[1024,4096]{1,0:T(8,128)(2,1)} %all-gather.7.cloned.1.call-done), kind=kOutput, calls=%fused_computation.33 | convolution fusion | flops 1612183552 | bytes 11153408 | tf_op jit(solution)/shard_map/dot_general | solution.py:14
  419.9 1.0 copy.15
  420.9 0.0 reduce-scatter.7.cloned.1.call-update
  420.9 0.0 reduce-scatter.5.cloned.1.call-start
  421.0 9.3 %convolution_multiply_fusion = f32[1024,4096]{1,0:T(8,128)} fusion(bf16[192,4096]{1,0:T(8,128)(2,1)S(1)} %copy-done, bf16[192,4096]{1,0:T(8,128)(2,1)S(1)} %fusion.1, bf16[192,1024]{1,0:T(8,128)(2,1)} %get-tuple-element.14, bf16[192,1024]{1,0:T(8,128)(2,1)S(1)} %get-tuple-element.21), kind=kOutput, calls=%fused_computation | convolution fusion | flops 3233284096 | bytes 20709376 | tf_op jit(solution)/shard_map/dot_general | solution.py:20
  430.3 0.0 reduce-scatter.5.cloned.1.call-update
  430.3 11.7 %reduce-scatter.7.cloned.1.call-done = f32[256,2]{1,0:T(8,128)} async-done(((f32[1024,2]{1,0:T(8,128)}), f32[256,2]{1,0:T(8,128)}) %reduce-scatter.7.cloned.1.call-update) | async-done | bytes 2064
  442.0 1.0 copy.16
  443.0 0.0 copy-done.6
  443.0 0.0 copy-done.7
  443.0 0.6 divide_subtract_fusion.1
  443.6 0.6 pad_maximum_fusion
  444.2 125.3 %reduce-scatter.5.cloned.1.call-done = f32[256,4096]{1,0:T(8,128)} async-done(((f32[1024,4096]{1,0:T(8,128)}), f32[256,4096]{1,0:T(8,128)}) %reduce-scatter.5.cloned.1.call-update) | async-done | bytes 4194320 | tf_op jit(solution)/shard_map/reduce_scatter | solution.py:83
  569.5 11.4 %divide_subtract_fusion = (f32[256,4096]{1,0:T(8,128)}, f32[256,4096]{1,0:T(8,128)}, f32[256,4096]{1,0:T(8,128)}) fusion(f32[256,4096]{1,0:T(8,128)} %param.12, f32[256,4096]{1,0:T(8,128)} %reduce-scatter.5.cloned.1.call-done, f32[256,4096]{1,0:T(8,128)} %param.14, f32[256,4096]{1,0:T(8,128)} %param.15), kind=kLoop, calls=%fused_computation.5 | loop fusion | flops 12582912 | bytes 29360128 | tf_op jit(solution)/shard_map/sub | solution.py:31
  (9 shorter events, 0.0 us)
Async XLA Ops:
  7.2 49.9 %all-gather.5.cloned.1.call-start = ((), (), s32[]{:S(2)}) async-start(), calls=%async_computation.2 | async-start | bytes 1769472 | tf_op jit(solution)/shard_map/all_gather | solution.py:45
  7.9 3.9 copy-start.2
  7.9 108.0 %all-gather.7.cloned.1.call-start = ((), (), s32[]{:S(2)}) async-start(), calls=%async_computation.3 | async-start | bytes 10485760 | tf_op jit(solution)/shard_map/all_gather | solution.py:47
  11.8 291.3 %all-gather.9.cloned.1.call-start = ((), (), s32[]{:S(2)}) async-start(), calls=%async_computation.6 | async-start | bytes 14155776 | tf_op jit(solution)/shard_map/all_gather | solution.py:58
  115.9 7.9 %copy-start.8 = (bf16[1024,4096]{1,0:T(8,128)(2,1)S(1)}, bf16[1024,4096]{1,0:T(8,128)(2,1)}, u32[]{:S(2)}) copy-start(bf16[1024,4096]{1,0:T(8,128)(2,1)} %all-gather.7.cloned.1.call-done) | copy-start | bytes 25165828
  123.8 3.1 copy-start.3
  126.8 283.2 %all-reduce.2.cloned.1.call-start = ((), (), s32[]{:S(2)}) async-start(), calls=%async_computation.4 | async-start | bytes 3145728 | tf_op jit(solution)/shard_map/psum | solution.py:67
  303.1 7.2 %copy-start = (bf16[192,4096]{1,0:T(8,128)(2,1)S(1)}, bf16[192,4096]{1,0:T(8,128)(2,1)}, u32[]{:S(2)}) copy-start(bf16[192,4096]{1,0:T(8,128)(2,1)} %all-gather.5.cloned.1.call-done) | copy-start | bytes 4718596
  303.1 7.2 %copy-start.4 = (f32[1,1024]{1,0:T(1,128)S(1)}, f32[1,1024]{1,0:T(1,128)}, u32[]{:S(2)}) copy-start(f32[1,1024]{1,0:T(1,128)} %get-tuple-element.15) | copy-start | bytes 12292
  303.1 7.2 %copy-start.5 = (f32[1,1024]{1,0:T(1,128)S(1)}, f32[1,1024]{1,0:T(1,128)}, u32[]{:S(2)}) copy-start(f32[1,1024]{1,0:T(1,128)} %get-tuple-element.16) | copy-start | bytes 12292
  310.2 12.1 %copy-start.1 = (bf16[192,4096]{1,0:T(8,128)(2,1)}, bf16[192,4096]{1,0:T(8,128)(2,1)S(1)}, u32[]{:S(2)}) copy-start(bf16[192,4096]{1,0:T(8,128)(2,1)S(1)} %reduce_sum.30) | copy-start | bytes 4718596
  322.4 119.7 %reduce-scatter.7.cloned.1.call-start = ((), (), s32[]{:S(2)}) async-start(), calls=%async_computation.7 | async-start | bytes 655360
  410.0 2.8 copy-start.9
  420.9 148.6 %reduce-scatter.5.cloned.1.call-start = ((), (), s32[]{:S(2)}) async-start(), calls=%async_computation.5 | async-start | bytes 20971520 | tf_op jit(solution)/shard_map/reduce_scatter | solution.py:83
  430.3 12.7 %copy-start.6 = (f32[2,256]{1,0:T(2,128)S(1)}, f32[2,256]{1,0:T(2,128)}, u32[]{:S(2)}) copy-start(f32[2,256]{1,0:T(2,128)} %param.16) | copy-start | bytes 6148
  430.3 12.7 %copy-start.7 = (f32[2,256]{1,0:T(2,128)S(1)}, f32[2,256]{1,0:T(2,128)}, u32[]{:S(2)}) copy-start(f32[2,256]{1,0:T(2,128)} %param.17) | copy-start | bytes 6148
Sparse Core Ops, SparseCore 0:
  10.2 46.8 all-gather.4
  59.2 56.6 all-gather.6
  126.9 176.0 all-gather.8
  322.5 87.4 all-reduce.1
  421.1 20.9 reduce-scatter.6
  444.5 125.0 reduce-scatter.4
